TPU v7x, 512 devices: a whole 4x8x8 slice. The times are simulated.
512 devices in a mesh: cfg: 2 (over z_lo), rs: 32 (over x, z_hi, core), tp: 8 (over y).
Axes of the slice: x: 4, y: 8, z: 8 (z_hi: 4, z_lo: 2; z = z_hi * 2 + z_lo), core: 2. Of those that a mesh axis runs over, the one named last changes fastest.
Arguments:
- latents: float32 [8192, 2, 16], P('rs'), may hold values from -6 to 6
- timesteps: int32 [8, 2], replicated, may hold values from 0 to 249
- labels: int32 [8, 2], replicated, may hold values from 0 to 999
- solver_table: float32 [250, 2], replicated, may hold values from 0.5 to 1.5
- time_table: bfloat16 [250, 1152], P(None, 'tp'), may hold values from -6 to 6
- label_table: bfloat16 [1001, 1152], P(None, 'tp'), may hold values from -6 to 6
- patch_weight: bfloat16 [16, 1152], replicated, may hold values from -1.5 to 1.5
- patch_bias: float32 [1152], replicated, may hold values from -3 to 3
- modulation_weight: bfloat16 [9216, 1152], P(('rs', 'tp')), may hold values from -0.1875 to 0.1875
- modulation_bias: float32 [9216], P(('rs', 'tp')), may hold values from -3 to 3
- heads_weight: bfloat16 [1, 1152, 3, 1152], P(None, None, None, 'tp'), may hold values from -0.375 to 0.375
- heads_bias: float32 [1, 3, 1152], P(None, None, 'tp'), may hold values from -1.75 to 1.75
- output_weight: bfloat16 [1, 1152, 1152], P(None, 'tp'), may hold values from -0.1875 to 0.1875
- output_bias: float32 [1, 1152], replicated, may hold values from -1.75 to 1.75
- up_weight: bfloat16 [1, 1152, 4608], P(None, None, 'tp'), may hold values from -0.1875 to 0.1875
- up_bias: float32 [1, 4608], P(None, 'tp'), may hold values from -1.75 to 1.75
- down_weight: bfloat16 [1, 4608, 1152], P(None, 'tp'), may hold values from -0.09375 to 0.09375
- down_bias: float32 [1, 1152], replicated, may hold values from -1.75 to 1.75
- final_weight: bfloat16 [1152, 16], replicated, may hold values from -0.1875 to 0.1875
- final_bias: float32 [16], replicated, may hold values from -1.75 to 1.75
Outputs:
- next_latents: float32 [8192, 2, 16], P(('rs', 'tp'), None, 'cfg')
All inputs are finite; a program needn't handle non-finite values.
Results may differ from a plain program's by a relative error of at most 0.02.
Values may be sent and summed in bfloat16 or wider, within the bound.
A program may use at most 64 MiB of HBM per device.

v0:
```python
import jax
import jax.numpy as jnp
from jax import lax
from jax.sharding import PartitionSpec as P

HEAD_DIM = 72
GRID = 32
LAYERS = 1
guidance = 4.0


def partner_2(value, axis, stride):
    mask = 2**stride
    pairs = [(source, source ^ mask) for source in range(lax.axis_size(axis))]
    return lax.ppermute(value, axis, pairs)


def layer_norm(values):
    centre = values - jnp.mean(values, axis=-1, keepdims=True)
    spread = jnp.mean(centre * centre, axis=-1, keepdims=True)
    return centre * lax.rsqrt(spread + 1e-06)


def position_rows(token_index, grid_side, model_width):
    freq_count = model_width // 4
    frequency = 1.0 / 10000.0 ** (jnp.arange(freq_count, dtype=jnp.float32) / freq_count)
    row_angle = (token_index // grid_side).astype(jnp.float32)[:, None] * frequency[None, :]
    col_angle = (token_index % grid_side).astype(jnp.float32)[:, None] * frequency[None, :]
    return jnp.concatenate(
        [jnp.sin(row_angle), jnp.cos(row_angle), jnp.sin(col_angle), jnp.cos(col_angle)], axis=1
    )


def modulate(stream, modulation, offset):
    return (
        layer_norm(stream) * (1.0 + modulation[None, :, offset + 1]) + modulation[None, :, offset]
    ).astype(jnp.bfloat16)


def project_heads(normed, weight, bias):
    row_count, latents_dev, model_width = normed.shape
    flattened = normed.reshape(row_count * latents_dev, model_width)
    result = jnp.dot(
        flattened, weight.reshape(model_width, -1), preferred_element_type=jnp.float32
    ) + bias.reshape(-1)
    return result.astype(jnp.bfloat16).reshape(row_count, latents_dev, -1)


def hidden_units(normed, weight, bias):
    row_count, latents_dev, model_width = normed.shape
    flattened = normed.reshape(row_count * latents_dev, model_width)
    preact = jnp.dot(flattened, weight, preferred_element_type=jnp.float32) + bias
    return (
        jax.nn.gelu(preact, approximate=True)
        .astype(jnp.bfloat16)
        .reshape(row_count, latents_dev, -1)
    )


def attend_block(queries, key_block, columns):
    key_count, latents_dev = (key_block.shape[0], key_block.shape[1])
    head_count, head_size = (queries.shape[2], queries.shape[3])
    key_rows = key_block[..., :columns].reshape(key_count, latents_dev, head_count, head_size)
    value_rows = key_block[..., columns:].reshape(key_count, latents_dev, head_count, head_size)
    scores = jnp.einsum(
        "qlhd,klhd->lhqk", queries, key_rows, preferred_element_type=jnp.float32
    ) * head_size ** (-0.5)
    row_top = jnp.max(scores, axis=-1)
    exponent = jnp.exp(scores - row_top[..., None])
    row_total = jnp.sum(exponent, axis=-1)
    weighted = jnp.einsum(
        "lhqk,klhd->lhqd",
        exponent.astype(jnp.bfloat16),
        value_rows,
        preferred_element_type=jnp.float32,
    )
    return (row_top, row_total, weighted)


def merge_blocks(first, second):
    row_top = jnp.maximum(first[0], second[0])
    left_scale = jnp.exp(first[0] - row_top)
    right_scale = jnp.exp(second[0] - row_top)
    row_total = first[1] * left_scale + second[1] * right_scale
    weighted = first[2] * left_scale[..., None] + second[2] * right_scale[..., None]
    return (row_top, row_total, weighted)


def attention(projected, columns, head_size):
    row_count, latents_dev = (projected.shape[0], projected.shape[1])
    queries = projected[..., :columns].reshape(
        row_count, latents_dev, columns // head_size, head_size
    )
    own_block = projected[..., columns:]
    running = attend_block(queries, own_block, columns)
    near_block = partner_2(own_block, "rs", 0)
    running = merge_blocks(running, attend_block(queries, near_block, columns))
    far_block = partner_2(jnp.concatenate([own_block, near_block], axis=0), "rs", 1)
    running = merge_blocks(running, attend_block(queries, far_block, columns))
    result = running[2] / running[1][..., None]
    return (
        jnp.transpose(result, (2, 0, 1, 3))
        .reshape(row_count, latents_dev, columns)
        .astype(jnp.bfloat16)
    )


def per_device(
    latents,
    timesteps,
    labels,
    solver_table,
    time_table,
    label_table,
    patch_weight,
    patch_bias,
    modulation_weight,
    modulation_bias,
    heads_weight,
    heads_bias,
    output_weight,
    output_bias,
    up_weight,
    up_bias,
    down_weight,
    down_bias,
    final_weight,
    final_bias,
):
    tp_count = lax.axis_size("tp")
    tp_index = lax.axis_index("tp")
    half_index = lax.axis_index("cfg")
    rs_index = lax.axis_index("rs")
    group_index = rs_index // 4
    quarter = rs_index % 4
    local_tokens, latents_dev, patch_width = latents.shape
    model_width = patch_weight.shape[1]
    share_rows = local_tokens // tp_count
    classes = label_table.shape[0] - 1
    columns = heads_weight.shape[3]
    steps_all = timesteps.reshape(-1)
    class_ids = jnp.where(half_index == 0, labels.reshape(-1), classes)
    step_onehot = jax.nn.one_hot(steps_all, time_table.shape[0], dtype=jnp.bfloat16)
    class_onehot = jax.nn.one_hot(class_ids, classes + 1, dtype=jnp.bfloat16)
    condition_part = jnp.dot(step_onehot, time_table, preferred_element_type=jnp.float32) + jnp.dot(
        class_onehot, label_table, preferred_element_type=jnp.float32
    )
    condition = lax.all_gather(condition_part, "tp", axis=1, tiled=True)
    activation = jax.nn.silu(condition).astype(jnp.bfloat16)
    modulation_part = (
        lax.dot_general(
            activation,
            modulation_weight,
            (((1,), (1,)), ((), ())),
            preferred_element_type=jnp.float32,
        )
        + modulation_bias
    )
    modulation_all = lax.all_gather(modulation_part, ("rs", "tp"), axis=1, tiled=True)
    modulation_all = modulation_all.reshape(timesteps.shape[0], latents_dev, -1, model_width)
    modulation = lax.dynamic_index_in_dim(modulation_all, group_index, 0, keepdims=False)
    token_index = quarter * local_tokens + jnp.arange(local_tokens, dtype=jnp.int32)
    position = position_rows(token_index, GRID, model_width)
    own_latents = lax.dynamic_slice_in_dim(latents, tp_index * share_rows, share_rows, 0)
    flattened = latents.reshape(-1, patch_width).astype(jnp.bfloat16)
    embedded = jnp.dot(flattened, patch_weight, preferred_element_type=jnp.float32) + patch_bias
    stream = embedded.reshape(latents.shape[0], latents_dev, model_width) + position[:, None, :]
    projected = project_heads(modulate(stream, modulation, 0), heads_weight[0], heads_bias[0])
    attended = attention(projected, columns, HEAD_DIM).reshape(-1, columns)
    head_terms = jnp.dot(attended, output_weight[0], preferred_element_type=jnp.float32)
    attn_out = (
        lax.psum(head_terms.astype(jnp.bfloat16), "tp")
        .astype(jnp.float32)
        .reshape(local_tokens, latents_dev, model_width)
    )
    stream = stream + modulation[None, :, 2] * (attn_out + output_bias[0])
    hidden = hidden_units(modulate(stream, modulation, 3), up_weight[0], up_bias[0])
    unit_terms = jnp.dot(
        hidden.reshape(-1, hidden.shape[2]), down_weight[0], preferred_element_type=jnp.float32
    )
    mlp_out = (
        lax.psum(unit_terms.astype(jnp.bfloat16), "tp")
        .astype(jnp.float32)
        .reshape(local_tokens, latents_dev, model_width)
    )
    stream = stream + modulation[None, :, 5] * (mlp_out + down_bias[0])
    own_stream = lax.dynamic_slice_in_dim(stream, tp_index * share_rows, share_rows, 0)
    final_normed = modulate(own_stream, modulation, 6 * LAYERS)
    noise_pred = (
        jnp.dot(
            final_normed.reshape(-1, model_width), final_weight, preferred_element_type=jnp.float32
        )
        + final_bias
    )
    noise_pred = noise_pred.reshape(share_rows, latents_dev, patch_width)
    half_width = patch_width // 2
    kept_half = lax.dynamic_slice_in_dim(noise_pred, half_index * half_width, half_width, 2)
    sent_half = lax.dynamic_slice_in_dim(noise_pred, (1 - half_index) * half_width, half_width, 2)
    partner = partner_2(sent_half, "cfg", 0)
    conditional = jnp.where(half_index == 0, kept_half, partner)
    unconditional = jnp.where(half_index == 0, partner, kept_half)
    guided = unconditional + guidance * (conditional - unconditional)
    own_channels = lax.dynamic_slice_in_dim(own_latents, half_index * half_width, half_width, 2)
    step_own = lax.dynamic_index_in_dim(timesteps, group_index, 0, keepdims=False)
    step_hot_own = jax.nn.one_hot(step_own, solver_table.shape[0], dtype=jnp.float32)
    coefficients = jnp.dot(step_hot_own, solver_table, precision=lax.Precision.HIGHEST)
    return coefficients[None, :, 0:1] * own_channels + coefficients[None, :, 1:2] * guided


def solution(mesh):
    in_specs = (
        P("rs", None, None),
        P(),
        P(),
        P(),
        P(None, "tp"),
        P(None, "tp"),
        P(),
        P(),
        P(("rs", "tp"), None),
        P(("rs", "tp")),
        P(None, None, None, "tp"),
        P(None, None, "tp"),
        P(None, "tp", None),
        P(),
        P(None, None, "tp"),
        P(None, "tp"),
        P(None, "tp", None),
        P(),
        P(),
        P(),
    )
    out_specs = P(("rs", "tp"), None, "cfg")
    return jax.shard_map(
        per_device, mesh=mesh, in_specs=in_specs, out_specs=out_specs, check_vma=False
    )
```

profile of v0, /device:TPU:2, one launch (start us, length us, event | category | flops | bytes accessed | tf_op | source)
XLA Modules:
  0.0 997.7 jit_solution(18414856131837989022)
XLA Ops:
  6.6 3.8 multiply_cosine_fusion
  12.0 2.2 add.308
  14.2 4.0 add.314
  18.4 3.6 fusion.90
  24.6 26.2 %all-gather = f32[8,144,16]{1,2,0:T(8,128)S(1)} all-gather(f32[1,144,16]{1,2,0:T(8,128)S(1)} %fusion.29), channel_id=1, replica_groups=mesh['cfg'=2,'rs'=32,'tp'=8] {'tp'}, dimensions={0}, use_global_device_ids=true | all-gather | bytes 82944 | tf_op jit(solution)/shard_map/all_gather | solution.py:148
  51.2 616.4 %all-gather.1 = f32[256,36,16]{1,2,0:T(8,128)S(1)} all-gather(f32[1,36,16]{1,2,0:T(8,128)S(1)} %fusion.30), channel_id=1, replica_groups=mesh['cfg'=2,'rs'=32,'tp'=8] {'rs','tp'}, dimensions={0}, use_global_device_ids=true | all-gather | bytes 592128 | tf_op jit(solution)/shard_map/all_gather | solution.py:159
  668.3 2.4 reshape.290
  674.7 4.0 add.321
  680.8 4.1 mul.285
  685.0 4.1 fusion.4
  696.1 2.2 pad_maximum_fusion
  700.4 2.1 collective-permute-start.1
  705.6 26.2 %collective-permute-done.1 = bf16[512,2,288]{0,2,1:T(8,128)(2,1)} collective-permute-done((bf16[512,2,288]{0,2,1:T(8,128)(2,1)}, bf16[512,2,288]{0,2,1:T(8,128)(2,1)}, u32[]{:S(2)}, u32[]{:S(2)}) %collective-permute-start.1) | collective-permute-done | bytes 589856 | tf_op jit(solution)/shard_map/ppermute | solution.py:15
  739.4 4.1 mul.306
  743.5 2.1 add.341
  745.6 4.0 add.342
  751.7 4.1 mul.312
  755.7 133.0 %all-reduce.3.cloned.1.call-done = bf16[512,1152]{1,0:T(8,128)(2,1)} async-done(((bf16[512,1152]{1,0:T(8,128)(2,1)}), bf16[512,1152]{1,0:T(8,128)(2,1)}) %all-reduce.3.cloned.1.call-update) | async-done | bytes 1179664 | tf_op jit(solution)/shard_map/psum | solution.py:172
  888.8 3.2 fusion.85
  893.7 5.7 convolution_convert_fusion.1
  901.0 4.1 reshape.272
  906.3 2.2 reshape.282
  908.5 73.4 %all-reduce.5.cloned.1.call-done = bf16[256,2,1152]{2,1,0:T(2,128)(2,1)} async-done(((bf16[256,2,1152]{2,1,0:T(2,128)(2,1)}), bf16[256,2,1152]{2,1,0:T(2,128)(2,1)}) %all-reduce.5.cloned.1.call-update) | async-done | bytes 1179664 | tf_op jit(solution)/shard_map/psum | solution.py:182
  984.7 3.6 collective-permute-start.2
  (144 shorter events, 42.9 us)
Async XLA Ops:
  6.5 887.2 %copy-start = (bf16[1,576,1152]{2,1,0:T(8,128)(2,1)S(1)}, bf16[1,576,1152]{2,1,0:T(8,128)(2,1)}, u32[]{:S(2)}) copy-start(bf16[1,576,1152]{2,1,0:T(8,128)(2,1)} %param.36) | copy-start | bytes 3981316
  6.5 882.2 %all-reduce.3.cloned.1.call-start = ((), (), s32[]{:S(2)}) async-start(), calls=%async_computation | async-start | bytes 2359296 | tf_op jit(solution)/shard_map/psum | solution.py:172
  12.0 6.3 copy-start.3
  14.2 4.1 copy-start.10
  14.2 4.2 copy-start.11
  14.2 4.2 copy-start.14
  22.1 2.3 copy-start.8
  22.1 28.9 %copy-start.22 = (bf16[36,1152]{1,0:T(8,128)(2,1)S(1)}, bf16[36,1152]{1,0:T(8,128)(2,1)}, u32[]{:S(2)}) copy-start(bf16[36,1152]{1,0:T(8,128)(2,1)} %param.28) | copy-start | bytes 248836
  22.1 28.9 %copy-start.26 = (f32[36]{0:T(128)S(1)}, f32[36]{0:T(128)}, u32[]{:S(2)}) copy-start(f32[36]{0:T(128)} %param.29) | copy-start | bytes 436
  680.8 4.1 copy-start.19
  680.8 4.2 copy-start.6
  690.2 5.9 copy-start.5
  690.2 5.9 collective-permute-start
  700.4 31.5 %collective-permute-start.1 = (bf16[512,2,288]{0,2,1:T(8,128)(2,1)}, bf16[512,2,288]{0,2,1:T(8,128)(2,1)}, u32[]{:S(2)}, u32[]{:S(2)}) collective-permute-start(bf16[512,2,288]{0,2,1:T(8,128)(2,1)} %copy.84), channel_id=1, source_target_pairs={{0,16},{8,24},{16,0},{24,8},{32,48},{40,56},{48,32},{56,40},{64,80... | collective-permute-start | bytes 1769480 | tf_op jit(solution)/shard_map/ppermute | solution.py:15
  737.3 244.6 %all-reduce.5.cloned.1.call-start = ((), (), s32[]{:S(2)}) async-start(), calls=%async_computation.1 | async-start | bytes 2359296 | tf_op jit(solution)/shard_map/psum | solution.py:182
  739.4 4.1 copy-start.15
  739.4 4.1 copy-start.12
  751.7 4.1 copy-start.20
  901.0 4.1 copy-start.16
  901.0 4.1 copy-start.25
  901.0 5.2 copy-start.4
  906.3 77.9 %copy-start.24 = (bf16[1152,16]{0,1:T(8,128)(2,1)S(1)}, bf16[1152,16]{0,1:T(8,128)(2,1)}, u32[]{:S(2)}) copy-start(bf16[1152,16]{0,1:T(8,128)(2,1)} %param.38) | copy-start | bytes 110596
  906.3 77.9 %copy-start.27 = (f32[16]{0:T(128)S(1)}, f32[16]{0:T(128)}, u32[]{:S(2)}) copy-start(f32[16]{0:T(128)} %param.39) | copy-start | bytes 196
  984.7 5.5 collective-permute-start.2
  (9 other events, 13.6 us)
Sparse Core Ops, SparseCore 0:
  737.4 151.2 all-reduce.2
  900.9 80.9 all-reduce.4
where the time goes:
time: 999 us; the launch traced here: 998 us
  blocking collectives  643 us (64%)
  waiting for transfers between devices  234 us (23%)
  local copies, waits for them, and re-layouts  64.7 us (6%)
  matrix products  19.2 us (2%)
  other arithmetic  15.1 us (2%)
  between operations  14 us (1%)
    all_gather x1, blocking collectives, per_device(): lax.all_gather(modulation_part, ('rs', 'tp'), axis=1, tiled=True)  616 us
    psum x1, waiting for transfers between devices, per_device(): lax.psum(head_terms.astype(jnp.bfloat16), 'tp').astype(jnp.float32)  133 us
    psum x1, waiting for transfers between devices, per_device(): lax.psum(unit_terms.astype(jnp.bfloat16), 'tp').astype(jnp.float32)  73.4 us
    ppermute x3, waiting for transfers between devices, partner_2(): return lax.ppermute(value, axis, pairs)  28 us
    all_gather x1, blocking collectives, per_device(): condition = lax.all_gather(condition_part, 'tp', axis=1, tiled=True)  26.2 us
  transfers between devices with their start and end apart: 5, of which 4 were waited for; matrix products, arithmetic and copies ran while one was open for 3% of the time, Pallas kernels for 0%

commit v1 on v0

--- a/solution.py
+++ b/solution.py
@@ -179,7 +179,7 @@
         hidden.reshape(-1, hidden.shape[2]), down_weight[0], preferred_element_type=jnp.float32
     )
     mlp_out = (
-        lax.psum(unit_terms.astype(jnp.bfloat16), "tp")
+        jnp.sum(lax.all_gather(unit_terms.astype(jnp.bfloat16), "tp"), axis=0)
         .astype(jnp.float32)
         .reshape(local_tokens, latents_dev, model_width)
     )

time: 999 us -> 1030 us (1.031)
  waiting for transfers between devices: 234 us -> 259 us
    all_gather x0 -> x1, waiting for transfers between devices: none -> 97.9 us  [per_device(): lax.all_gather(unit_terms.astype(jnp.bfloat16), 'tp')]
    psum x1 -> x0, waiting for transfers between devices: 73.4 us -> none  [per_device(): lax.psum(unit_terms.astype(jnp.bfloat16), 'tp').astype(jnp.float32)]
where the time goes in v1:
time: 1030 us
  blocking collectives  643 us (62%)
  waiting for transfers between devices  259 us (25%)
  local copies, waits for them, and re-layouts  66 us (6%)
  other arithmetic  20.8 us (2%)
  matrix products  20 us (2%)
  between operations  14 us (1%)
    all_gather x1, blocking collectives, per_device(): lax.all_gather(modulation_part, ('rs', 'tp'), axis=1, tiled=True)  616 us
    psum x1, waiting for transfers between devices, per_device(): lax.psum(head_terms.astype(jnp.bfloat16), 'tp').astype(jnp.float32)  133 us
    all_gather x1, waiting for transfers between devices, per_device(): lax.all_gather(unit_terms.astype(jnp.bfloat16), 'tp')  97.9 us
    ppermute x3, waiting for transfers between devices, partner_2(): return lax.ppermute(value, axis, pairs)  28 us
    all_gather x1, blocking collectives, per_device(): condition = lax.all_gather(condition_part, 'tp', axis=1, tiled=True)  26.2 us
  transfers between devices with their start and end apart: 5, of which 4 were waited for; matrix products, arithmetic and copies ran while one was open for 3% of the time, Pallas kernels for 0%

profile of v1, /device:TPU:2, one launch (start us, length us, event | category | flops | bytes accessed | tf_op | source)
XLA Modules:
  0.0 1030.0 jit_solution(2793520905622703950)
XLA Ops:
  6.6 3.8 multiply_cosine_fusion
  12.0 2.2 add.306
  14.2 4.0 add.312
  18.4 3.6 fusion.91
  24.6 26.2 %all-gather.1 = f32[8,144,16]{1,2,0:T(8,128)S(1)} all-gather(f32[1,144,16]{1,2,0:T(8,128)S(1)} %fusion.29), channel_id=1, replica_groups=mesh['cfg'=2,'rs'=32,'tp'=8] {'tp'}, dimensions={0}, use_global_device_ids=true | all-gather | bytes 82944 | tf_op jit(solution)/shard_map/all_gather | solution.py:148
  51.2 616.4 %all-gather.2 = f32[256,36,16]{1,2,0:T(8,128)S(1)} all-gather(f32[1,36,16]{1,2,0:T(8,128)S(1)} %fusion.30), channel_id=1, replica_groups=mesh['cfg'=2,'rs'=32,'tp'=8] {'rs','tp'}, dimensions={0}, use_global_device_ids=true | all-gather | bytes 592128 | tf_op jit(solution)/shard_map/all_gather | solution.py:159
  668.3 2.4 reshape.288
  674.7 4.0 add.319
  680.8 4.1 mul.285
  685.0 4.1 fusion.4
  696.1 2.2 pad_maximum_fusion
  705.6 26.2 %collective-permute-done.1 = bf16[512,2,288]{0,2,1:T(8,128)(2,1)} collective-permute-done((bf16[512,2,288]{0,2,1:T(8,128)(2,1)}, bf16[512,2,288]{0,2,1:T(8,128)(2,1)}, u32[]{:S(2)}, u32[]{:S(2)}) %collective-permute-start.1) | collective-permute-done | bytes 589856 | tf_op jit(solution)/shard_map/ppermute | solution.py:15
  739.4 4.1 mul.306
  745.6 4.0 add.340
  751.6 4.1 mul.312
  755.7 133.1 %all-reduce.2.cloned.1.call-done = bf16[512,1152]{1,0:T(8,128)(2,1)} async-done(((bf16[512,1152]{1,0:T(8,128)(2,1)}), bf16[512,1152]{1,0:T(8,128)(2,1)}) %all-reduce.2.cloned.1.call-update) | async-done | bytes 1179664 | tf_op jit(solution)/shard_map/psum | solution.py:172
  888.8 3.2 fusion.86
  894.1 6.4 convolution_convert_fusion.1
  900.8 4.0 reshape.270
  906.0 2.2 reshape.280
  908.3 97.9 %all-gather.5.cloned.1.call-done = bf16[4096,1152]{1,0:T(8,128)(2,1)} async-done(((bf16[512,1152]{1,0:T(8,128)(2,1)}), bf16[4096,1152]{1,0:T(8,128)(2,1)}) %all-gather.5.cloned.1.call-update) | async-done | bytes 9437200 | tf_op jit(solution)/shard_map/all_gather | solution.py:182
  1006.2 5.7 reduce_sum.109
  1011.9 2.2 reshape.283
  1016.9 3.6 collective-permute-start.2
  (146 shorter events, 46.1 us)
Async XLA Ops:
  6.5 887.2 %copy-start = (bf16[1,576,1152]{2,1,0:T(8,128)(2,1)S(1)}, bf16[1,576,1152]{2,1,0:T(8,128)(2,1)}, u32[]{:S(2)}) copy-start(bf16[1,576,1152]{2,1,0:T(8,128)(2,1)} %param.36) | copy-start | bytes 3981316
  6.5 882.3 %all-reduce.2.cloned.1.call-start = ((), (), s32[]{:S(2)}) async-start(), calls=%async_computation | async-start | bytes 2359296 | tf_op jit(solution)/shard_map/psum | solution.py:172
  12.0 6.3 copy-start.3
  14.2 4.1 copy-start.10
  14.2 4.2 copy-start.11
  14.2 4.2 copy-start.14
  22.1 2.3 copy-start.8
  22.1 28.9 %copy-start.23 = (bf16[36,1152]{1,0:T(8,128)(2,1)S(1)}, bf16[36,1152]{1,0:T(8,128)(2,1)}, u32[]{:S(2)}) copy-start(bf16[36,1152]{1,0:T(8,128)(2,1)} %param.28) | copy-start | bytes 248836
  22.1 28.9 %copy-start.27 = (f32[36]{0:T(128)S(1)}, f32[36]{0:T(128)}, u32[]{:S(2)}) copy-start(f32[36]{0:T(128)} %param.29) | copy-start | bytes 436
  680.8 4.1 copy-start.19
  680.8 4.2 copy-start.6
  690.2 5.9 copy-start.5
  690.2 5.9 collective-permute-start
  700.4 31.5 %collective-permute-start.1 = (bf16[512,2,288]{0,2,1:T(8,128)(2,1)}, bf16[512,2,288]{0,2,1:T(8,128)(2,1)}, u32[]{:S(2)}, u32[]{:S(2)}) collective-permute-start(bf16[512,2,288]{0,2,1:T(8,128)(2,1)} %copy.84), channel_id=1, source_target_pairs={{0,16},{8,24},{16,0},{24,8},{32,48},{40,56},{48,32},{56,40},{64,80... | collective-permute-start | bytes 1769480 | tf_op jit(solution)/shard_map/ppermute | solution.py:15
  737.3 268.9 %all-gather.5.cloned.1.call-start = ((), (), s32[]{:S(2)}) async-start(), calls=%async_computation.1 | async-start | bytes 10616832 | tf_op jit(solution)/shard_map/all_gather | solution.py:182
  739.4 4.1 copy-start.15
  751.6 4.1 copy-start.20
  894.1 6.5 copy-start.18
  900.8 4.0 copy-start.16
  900.8 4.1 copy-start.26
  900.8 5.2 copy-start.4
  1011.9 4.5 copy-start.25
  1011.9 4.5 copy-start.28
  1016.9 5.5 collective-permute-start.2
  (10 other events, 16.4 us)
Sparse Core Ops, SparseCore 0:
  737.4 151.3 all-reduce.1
  900.7 105.4 all-gather.4
